TPU v7x, 256 devices: a whole 4x4x8 slice. The times are simulated.
256 devices in a mesh: imp: 32 (over z, y_hi, core), cre: 8 (over x, y_lo).
Axes of the slice: x: 4, y: 4 (y_hi: 2, y_lo: 2; y = y_hi * 2 + y_lo), z: 8, core: 2. Of those that a mesh axis runs over, the one named last changes fastest.
Arguments:
- impressions: bfloat16 [32768, 256], P('imp'), may hold values from -24 to 24
- panels: bfloat16 [8, 2048, 256], P('cre', 'imp'), may hold values from -2 to 2
- block_lists: int32 [256, 16], P('imp'), may hold values from 0 to 127, as said below
- block_counts: int32 [256], P('imp'), may hold values from 1 to 16, as said below
- imp_weight: float32 [32768], P('imp'), may hold values from 0.2 to 5
- spend_goals: float32 [8, 2048], P('cre', 'imp'), may hold values from 0.2 to 5
- prices: float32 [8, 2048], P('cre', 'imp'), may hold values from -1 to 1
Outputs:
- final_prices: float32 [8, 2048], P('cre', 'imp')
- final_spend: float32 [8, 2048], P('cre', 'imp')
- log_norm: float32 [32768], P('imp')
Inputs may be any that keep to these rules, and one draw needn't show every extreme that they name: `block_lists`: each row lists 16 different block ids; only the first block_counts entries of a row are eligible for the 128 impressions of that tile, the others must be ignored. `block_counts`: some tile has 16 eligible blocks.
All inputs are finite; a program needn't handle non-finite values.
Results may differ from a plain program's by a relative error of at most 0.0003.
Values may be sent and summed in bfloat16 or wider, within the bound.
A program may use at most 64 MiB of HBM per device.

v0:
```python
import jax
import jax.numpy as jnp
from jax import lax
from jax.sharding import PartitionSpec as P

CRE_LOC = 2048
TILE = 128
BLOCK = 128
ITERS = 2
NEG_FILL = -1e30
TAU_INV = 4.0
STEP_RATE = 0.5


def block_table(block_lists, block_counts, local_blocks, cre_index):
    block_ids = cre_index * local_blocks + lax.iota(jnp.int32, local_blocks)
    in_list = lax.iota(jnp.int32, block_lists.shape[1])[None, :] < block_counts[:, None]
    matches = (block_lists[:, :, None] == block_ids[None, None, :]) & in_list[:, :, None]
    allowed = jnp.any(matches, axis=1)
    allowed = jnp.repeat(allowed, TILE, axis=0)
    return jnp.repeat(allowed, BLOCK, axis=1)


def scored(impressions, panel_rows, price_rows, col_mask):
    affinity = lax.dot_general(
        impressions, panel_rows, (((1,), (1,)), ((), ())), preferred_element_type=jnp.float32
    )
    logit_vals = TAU_INV * affinity + price_rows[None, :]
    return jnp.where(col_mask, logit_vals, NEG_FILL)


def sweep(panel_rows, group_prices, mask_full, running, update):
    col_count = panel_rows.shape[0]
    sub_width = 512

    def inner(current, step_index):
        shift_cols = step_index * sub_width
        part_panel = lax.dynamic_slice_in_dim(panel_rows, shift_cols, sub_width, 0)
        part_price = lax.dynamic_slice_in_dim(group_prices, shift_cols, sub_width, 0)
        part_mask = lax.dynamic_slice_in_dim(mask_full, shift_cols, sub_width, 1)
        return (update(current, part_panel, part_price, part_mask, shift_cols), None)

    current, _ = lax.scan(inner, running, jnp.arange(col_count // sub_width, dtype=jnp.int32))
    return current


def shards(impressions, panels, block_lists, block_counts, imp_weight, spend_goals, prices):
    local_blocks = CRE_LOC // BLOCK
    mask_full = block_table(block_lists, block_counts, local_blocks, lax.axis_index("cre"))
    imp_rows = impressions.shape[0]
    owned_rows = prices.shape[1]
    owned_start = lax.axis_index("imp") * owned_rows

    def max_step(current, panel_rows, price_rows, col_mask, first_col):
        row_top, row_total = current
        masked = scored(impressions, panel_rows, price_rows, col_mask)
        block_top = jnp.max(masked, axis=1)
        new_top = jnp.maximum(row_top, block_top)
        block_sum = jnp.sum(jnp.where(col_mask, jnp.exp(masked - block_top[:, None]), 0.0), axis=1)
        return (
            new_top,
            row_total * jnp.exp(row_top - new_top) + block_sum * jnp.exp(block_top - new_top),
        )

    spend_owned = None
    row_norm = None
    for iteration in range(ITERS):
        start_state = (
            jnp.full((imp_rows,), NEG_FILL, jnp.float32),
            jnp.zeros((imp_rows,), jnp.float32),
        )
        empty_spend = jnp.zeros((CRE_LOC,), jnp.float32)
        whole_prices = lax.all_gather(prices, "imp", axis=1, tiled=True)[0]
        row_top, row_total = sweep(
            lax.all_gather(panels, "imp", axis=1, tiled=True)[0],
            whole_prices,
            mask_full,
            start_state,
            max_step,
        )
        merged_top = lax.pmax(row_top, "cre")
        row_total = lax.psum(row_total * jnp.exp(row_top - merged_top), "cre")
        row_top = merged_top
        row_norm = row_top + jnp.log(row_total)

        def spend_step(current, panel_rows, price_rows, col_mask, first_col):
            masked = scored(impressions, panel_rows, price_rows, col_mask)
            shares = jnp.where(col_mask, jnp.exp(masked - row_norm[:, None]), 0.0)
            col_spend = jnp.sum(imp_weight[:, None] * shares, axis=0)
            return lax.dynamic_update_slice_in_dim(current, col_spend, first_col, 0)

        partial_spend = sweep(
            lax.all_gather(panels, "imp", axis=1, tiled=True)[0],
            whole_prices,
            mask_full,
            empty_spend,
            spend_step,
        )
        summed = lax.psum(partial_spend, "imp")
        spend_owned = lax.dynamic_slice_in_dim(summed, owned_start, owned_rows, 0)
        spend_owned = spend_owned.reshape(1, owned_rows)
        prices = prices + STEP_RATE * (
            jnp.log(spend_goals) - jnp.log(spend_owned + 0.25 * spend_goals)
        )
    return (prices, spend_owned, row_norm)


def solution(mesh):
    placed = (
        P("imp", None),
        P("cre", "imp", None),
        P("imp", None),
        P("imp"),
        P("imp"),
        P("cre", "imp"),
        P("cre", "imp"),
    )
    return jax.shard_map(
        shards,
        mesh=mesh,
        in_specs=placed,
        out_specs=(P("cre", "imp"), P("cre", "imp"), P("imp")),
        check_vma=False,
    )
```

profile of v0, /device:TPU:1, one launch (start us, length us, event | category | flops | bytes accessed | tf_op | source)
XLA Modules:
  0.0 427.9 jit_solution(15510092804575440473)
XLA Ops:
  7.2 0.7 all-gather.2.cloned.1.call-update
  8.0 0.7 iota_compare_fusion
  8.7 0.8 and_reduce_fusion
  9.7 1.3 dynamic-slice
  11.6 0.8 bitcast_dynamic-update-slice_fusion.1
  12.4 70.3 %all-reduce = f32[2048]{0:T(1024)S(1)} all-reduce(f32[2048]{0:T(1024)S(1)} %bitcast_dynamic-update-slice_fusion.1), channel_id=1, replica_groups=mesh['imp'=32,'cre'=8] {'imp'}, use_global_device_ids=true, to_apply=%add | all-reduce | flops 2048 | bytes 16384 | tf_op jit(solution)/shard_map/squeeze | solution.py:73
  82.8 9.8 %all-gather.2.cloned.1.call-done = bf16[1,2048,256]{2,1,0:T(8,128)(2,1)} async-done(((bf16[1,64,256]{2,1,0:T(8,128)(2,1)}), bf16[1,2048,256]{2,1,0:T(8,128)(2,1)}) %all-gather.2.cloned.1.call-update) | async-done | bytes 1048592 | tf_op jit(solution)/shard_map/all_gather | solution.py:93
  92.5 0.5 broadcast_in_dim.47
  93.1 0.7 copy-done.3
  93.7 15.7 %while.48 = (s32[]{:T(128)}, f32[1024]{0:T(1024)S(1)}, f32[1024]{0:T(1024)S(1)}, s32[4]{0:T(128)S(1)}, pred[1024,2048]{0,1:T(32,128)(4,1)S(1)}, /*index=5*/bf16[...) while((s32[]{:T(128)}, f32[1024]{0:T(1024)S(1)}, ...), condition=%wide.region_4.5_spmd.clone, body=%wide.region_1.4_spmd.clone.sunk | while | flops 273684480 | bytes 6075585 | solution.py:43
  93.8 0.7 dynamic_slice.118
  95.2 1.7 fusion.49
  96.9 0.8 select_reduce_fusion.4
  97.7 0.7 dynamic_slice.118
  99.1 1.7 fusion.49
  100.8 0.8 select_reduce_fusion.4
  101.6 0.7 dynamic_slice.118
  103.0 1.7 fusion.49
  104.7 0.8 select_reduce_fusion.4
  105.5 0.7 dynamic_slice.118
  107.0 1.7 fusion.49
  108.6 0.8 select_reduce_fusion.4
  109.4 14.9 %pmax.14 = f32[1024]{0:T(1024)S(1)} all-reduce(f32[1024]{0:T(1024)S(1)} %get-tuple-element.183), channel_id=1, replica_groups=mesh['imp'=32,'cre'=8] {'cre'}, use_global_device_ids=true, to_apply=%region_5.6 | all-reduce | flops 1024 | bytes 8192 | tf_op jit(solution)/shard_map/pmax | solution.py:81
  124.4 12.5 %psum.28 = f32[1024]{0:T(1024)S(1)} all-reduce(f32[1024]{0:T(1024)S(1)} %exponential_multiply_fusion.1), channel_id=1, replica_groups=mesh['imp'=32,'cre'=8] {'cre'}, use_global_device_ids=true, to_apply=%region_6.7 | all-reduce | flops 1024 | bytes 8192 | tf_op jit(solution)/shard_map/psum | solution.py:82
  136.9 14.6 %while.46 = (s32[]{:T(128)}, f32[2048]{0:T(1024)S(1)}, f32[1024]{0:T(1024)S(1)}, s32[4]{0:T(128)S(1)}, pred[1024,2048]{0,1:T(32,128)(4,1)S(1)}, /*index=5*/bf16[...) while((s32[]{:T(128)}, f32[2048]{0:T(1024)S(1)}, ...), condition=%wide.region_9.10_spmd, body=%wide.region_7.9_spmd.sunk | while | flops 272104960 | bytes 1332415 | solution.py:43
  136.9 0.6 dynamic_slice.109
  138.2 2.1 fusion.44
  140.3 0.3 dynamic_update_slice.8
  140.6 0.6 dynamic_slice.109
  141.9 2.1 fusion.44
  144.0 0.3 dynamic_update_slice.8
  144.2 0.6 dynamic_slice.109
  145.6 2.1 fusion.44
  147.9 0.6 dynamic_slice.109
  149.2 2.1 fusion.44
  151.5 72.9 %psum.29 = f32[2048]{0:T(1024)S(1)} all-reduce(f32[2048]{0:T(1024)S(1)} %get-tuple-element.185), channel_id=1, replica_groups=mesh['imp'=32,'cre'=8] {'imp'}, use_global_device_ids=true, to_apply=%region_10.11 | all-reduce | flops 2048 | bytes 16384 | tf_op jit(solution)/shard_map/psum | solution.py:99
  224.6 66.0 %all-reduce.1 = f32[2048]{0:T(1024)S(1)} all-reduce(f32[2048]{0:T(1024)S(1)} %get-tuple-element.317), channel_id=1, replica_groups=mesh['imp'=32,'cre'=8] {'imp'}, use_global_device_ids=true, to_apply=%add.1 | all-reduce | flops 2048 | bytes 16384 | tf_op jit(solution)/shard_map/squeeze | solution.py:73
  290.7 15.2 %while.49 = (s32[]{:T(128)}, f32[1024]{0:T(1024)S(1)}, f32[1024]{0:T(1024)S(1)}, s32[4]{0:T(128)S(1)}, pred[1024,2048]{0,1:T(32,128)(4,1)S(1)}, /*index=5*/bf16[...) while((s32[]{:T(128)}, f32[1024]{0:T(1024)S(1)}, ...), condition=%wide.region_14.15_spmd.clone, body=%wide.region_11.14_spmd.clone.sunk | while | flops 273684480 | bytes 6075585 | solution.py:43
  290.7 0.6 dynamic_slice.123
  292.0 1.7 fusion.52
  293.7 0.8 select_reduce_fusion.5
  294.5 0.6 dynamic_slice.123
  295.8 1.7 fusion.52
  297.5 0.8 select_reduce_fusion.5
  298.3 0.6 dynamic_slice.123
  299.6 1.7 fusion.52
  301.3 0.8 select_reduce_fusion.5
  302.1 0.6 dynamic_slice.123
  303.4 1.7 fusion.52
  305.1 0.8 select_reduce_fusion.5
  305.9 14.2 %pmax.15 = f32[1024]{0:T(1024)S(1)} all-reduce(f32[1024]{0:T(1024)S(1)} %get-tuple-element.186), channel_id=1, replica_groups=mesh['imp'=32,'cre'=8] {'cre'}, use_global_device_ids=true, to_apply=%region_15.16 | all-reduce | flops 1024 | bytes 8192 | tf_op jit(solution)/shard_map/pmax | solution.py:81
  320.0 12.8 %psum.30 = f32[1024]{0:T(1024)S(1)} all-reduce(f32[1024]{0:T(1024)S(1)} %exponential_multiply_fusion), channel_id=1, replica_groups=mesh['imp'=32,'cre'=8] {'cre'}, use_global_device_ids=true, to_apply=%region_16.17 | all-reduce | flops 1024 | bytes 8192 | tf_op jit(solution)/shard_map/psum | solution.py:82
  332.8 14.6 %while.47 = (s32[]{:T(128)}, f32[2048]{0:T(1024)S(1)}, f32[1024]{0:T(1024)S(1)}, s32[4]{0:T(128)S(1)}, pred[1024,2048]{0,1:T(32,128)(4,1)S(1)}, /*index=5*/bf16[...) while((s32[]{:T(128)}, f32[2048]{0:T(1024)S(1)}, ...), condition=%wide.region_19.20_spmd, body=%wide.region_17.19_spmd.sunk | while | flops 272104960 | bytes 1332415 | solution.py:43
  332.8 0.6 dynamic_slice.113
  334.1 2.1 fusion.47
  336.2 0.3 dynamic_update_slice.9
  336.5 0.6 dynamic_slice.113
  337.8 2.1 fusion.47
  340.2 0.6 dynamic_slice.113
  341.5 2.1 fusion.47
  343.8 0.6 dynamic_slice.113
  345.1 2.1 fusion.47
  347.4 73.0 %psum.31 = f32[2048]{0:T(1024)S(1)} all-reduce(f32[2048]{0:T(1024)S(1)} %get-tuple-element.188), channel_id=1, replica_groups=mesh['imp'=32,'cre'=8] {'imp'}, use_global_device_ids=true, to_apply=%region_20.21 | all-reduce | flops 2048 | bytes 16384 | tf_op jit(solution)/shard_map/psum | solution.py:99
  420.5 0.6 multiply_add_fusion
  (60 shorter events, 3.1 us)
Async XLA Ops:
  7.2 85.4 %all-gather.2.cloned.1.call-start = ((), (), s32[]{:S(2)}) async-start(), calls=%async_computation | async-start | bytes 1081344 | tf_op jit(solution)/shard_map/all_gather | solution.py:93
  92.5 1.2 copy-start.3
  93.7 43.1 %copy-start.4 = (f32[1024]{0:T(1024)S(1)}, f32[1024]{0:T(1024)}, u32[]{:S(2)}) copy-start(f32[1024]{0:T(1024)} %param.19) | copy-start | bytes 12292
  136.9 87.5 %copy-start.1 = (f32[1,64]{1,0:T(1,128)S(1)}, f32[1,64]{1,0:T(1,128)}, u32[]{:S(2)}) copy-start(f32[1,64]{1,0:T(1,128)} %param.20) | copy-start | bytes 772
  136.9 87.5 %copy-start.2 = (f32[1,64]{1,0:T(1,128)S(1)}, f32[1,64]{1,0:T(1,128)}, u32[]{:S(2)}) copy-start(f32[1,64]{1,0:T(1,128)} %param.21) | copy-start | bytes 772
  347.4 73.7 %copy-start = (f32[1024]{0:T(1024)}, f32[1024]{0:T(1024)S(1)}, u32[]{:S(2)}) copy-start(f32[1024]{0:T(1024)S(1)} %get-tuple-element.705) | copy-start | bytes 12292
Sparse Core Ops, SparseCore 0:
  10.8 81.6 all-gather.1
where the time goes:
time: 429 us; the launch traced here: 428 us
  blocking collectives  337 us (79%)
  matrix products  29.8 us (7%)
  local copies, waits for them, and re-layouts  16.5 us (4%)
  between operations  14.9 us (3%)
  loops' own time  11 us (3%)
  waiting for transfers between devices  10.4 us (2%)
  other arithmetic  8.58 us (2%)
    psum x2, blocking collectives, shards(): summed = lax.psum(partial_spend, 'imp')  146 us
    squeeze x2, blocking collectives, shards(): whole_prices = lax.all_gather(prices, 'imp', axis=1, tiled=True)[0]  136 us
    dot_general x16, matrix products, scored(): lax.dot_general(impressions, panel_rows, (((1,), (1,)), ((), ())), prefer...  29.8 us
    pmax x2, blocking collectives, shards(): merged_top = lax.pmax(row_top, 'cre')  29.1 us
    psum x2, blocking collectives, shards(): row_total = lax.psum(row_total * jnp.exp(row_top - merged_top), 'cre')  25.2 us
    another operation x4, loops' own time, sweep(): lax.scan(inner, running, jnp.arange(col_count // sub_width, dtype=jnp.int...  11 us
    all_gather x1, waiting for transfers between devices, shards(): lax.all_gather(panels, 'imp', axis=1, tiled=True)[0]  9.76 us
    dynamic_slice x16, local copies, waits for them, and re-layouts, sweep(): lax.scan(inner, running, jnp.arange(col_count // sub_width, dtype=jnp.int...  9.67 us
  transfers between devices with their start and end apart: 1, of which 1 were waited for; matrix products, arithmetic and copies ran while one was open for 1% of the time, Pallas kernels for 0%

commit v1 on v0

--- a/solution.py
+++ b/solution.py
@@ -79,7 +79,9 @@
             max_step,
         )
         merged_top = lax.pmax(row_top, "cre")
-        row_total = lax.psum(row_total * jnp.exp(row_top - merged_top), "cre")
+        row_total = jnp.sum(
+            lax.all_gather(row_total * jnp.exp(row_top - merged_top), "cre"), axis=0
+        )
         row_top = merged_top
         row_norm = row_top + jnp.log(row_total)
 

time: 429 us -> 451 us (1.051)
  blocking collectives: 337 us -> 359 us
    all_gather x0 -> x2, blocking collectives: none -> 43.4 us  [shards(): lax.all_gather(row_total * jnp.exp(row_top - merged_top), 'cre')]
    psum x2 -> x0, blocking collectives: 25.2 us -> none  [shards(): row_total = lax.psum(row_total * jnp.exp(row_top - merged_top), 'cre')]
    psum x2, blocking collectives: 146 us -> 152 us  [shards(): summed = lax.psum(partial_spend, 'imp')]
where the time goes in v1:
time: 451 us; the launch traced here: 450 us
  blocking collectives  359 us (80%)
  matrix products  29.8 us (7%)
  local copies, waits for them, and re-layouts  16.5 us (4%)
  between operations  14.9 us (3%)
  loops' own time  11 us (2%)
  waiting for transfers between devices  10.4 us (2%)
  other arithmetic  8.59 us (2%)
    psum x2, blocking collectives, shards(): summed = lax.psum(partial_spend, 'imp')  152 us
    squeeze x2, blocking collectives, shards(): whole_prices = lax.all_gather(prices, 'imp', axis=1, tiled=True)[0]  136 us
    all_gather x2, blocking collectives, shards(): lax.all_gather(row_total * jnp.exp(row_top - merged_top), 'cre')  43.4 us
    dot_general x16, matrix products, scored(): lax.dot_general(impressions, panel_rows, (((1,), (1,)), ((), ())), prefer...  29.8 us
    pmax x2, blocking collectives, shards(): merged_top = lax.pmax(row_top, 'cre')  27.4 us
    another operation x4, loops' own time, sweep(): lax.scan(inner, running, jnp.arange(col_count // sub_width, dtype=jnp.int...  11 us
    all_gather x1, waiting for transfers between devices, shards(): lax.all_gather(panels, 'imp', axis=1, tiled=True)[0]  9.76 us
    dynamic_slice x16, local copies, waits for them, and re-layouts, sweep(): lax.scan(inner, running, jnp.arange(col_count // sub_width, dtype=jnp.int...  9.67 us
  transfers between devices with their start and end apart: 1, of which 1 were waited for; matrix products, arithmetic and copies ran while one was open for 1% of the time, Pallas kernels for 0%

profile of v1, /device:TPU:1, one launch (start us, length us, event | category | flops | bytes accessed | tf_op | source)
XLA Modules:
  0.0 450.2 jit_solution(1288529005281568920)
XLA Ops:
  7.2 0.7 all-gather.4.cloned.1.call-update
  8.0 0.7 iota_compare_fusion
  8.7 0.8 and_reduce_fusion
  9.7 1.3 dynamic-slice
  11.6 0.8 bitcast_dynamic-update-slice_fusion.1
  12.4 70.3 %all-reduce = f32[2048]{0:T(1024)S(1)} all-reduce(f32[2048]{0:T(1024)S(1)} %bitcast_dynamic-update-slice_fusion.1), channel_id=1, replica_groups=mesh['imp'=32,'cre'=8] {'imp'}, use_global_device_ids=true, to_apply=%add | all-reduce | flops 2048 | bytes 16384 | tf_op jit(solution)/shard_map/squeeze | solution.py:73
  82.8 9.8 %all-gather.4.cloned.1.call-done = bf16[1,2048,256]{2,1,0:T(8,128)(2,1)} async-done(((bf16[1,64,256]{2,1,0:T(8,128)(2,1)}), bf16[1,2048,256]{2,1,0:T(8,128)(2,1)}) %all-gather.4.cloned.1.call-update) | async-done | bytes 1048592 | tf_op jit(solution)/shard_map/all_gather | solution.py:95
  92.5 0.5 broadcast_in_dim.47
  93.1 0.7 copy-done.3
  93.7 15.7 %while.48 = (s32[]{:T(128)}, f32[1024]{0:T(1024)S(1)}, f32[1024]{0:T(1024)S(1)}, s32[4]{0:T(128)S(1)}, pred[1024,2048]{0,1:T(32,128)(4,1)S(1)}, /*index=5*/bf16[...) while((s32[]{:T(128)}, f32[1024]{0:T(1024)S(1)}, ...), condition=%wide.region_4.5_spmd.clone, body=%wide.region_1.4_spmd.clone.sunk | while | flops 273684480 | bytes 6075585 | solution.py:43
  93.8 0.7 dynamic_slice.118
  95.2 1.7 fusion.49
  96.9 0.8 select_reduce_fusion.4
  97.7 0.7 dynamic_slice.118
  99.1 1.7 fusion.49
  100.8 0.8 select_reduce_fusion.4
  101.6 0.7 dynamic_slice.118
  103.0 1.7 fusion.49
  104.7 0.8 select_reduce_fusion.4
  105.5 0.7 dynamic_slice.118
  106.9 1.7 fusion.49
  108.6 0.8 select_reduce_fusion.4
  109.4 14.9 %pmax.14 = f32[1024]{0:T(1024)S(1)} all-reduce(f32[1024]{0:T(1024)S(1)} %get-tuple-element.183), channel_id=1, replica_groups=mesh['imp'=32,'cre'=8] {'cre'}, use_global_device_ids=true, to_apply=%region_5.6 | all-reduce | flops 1024 | bytes 8192 | tf_op jit(solution)/shard_map/pmax | solution.py:81
  124.3 21.7 %all-gather = f32[8192]{0:T(1024)S(1)} all-gather(f32[1024]{0:T(1024)S(1)} %exponential_multiply_fusion.1), channel_id=2, replica_groups=mesh['imp'=32,'cre'=8] {'cre'}, dimensions={0}, use_global_device_ids=true | all-gather | bytes 36864 | tf_op jit(solution)/shard_map/all_gather | solution.py:83
  146.1 14.6 %while.46 = (s32[]{:T(128)}, f32[2048]{0:T(1024)S(1)}, f32[1024]{0:T(1024)S(1)}, s32[4]{0:T(128)S(1)}, pred[1024,2048]{0,1:T(32,128)(4,1)S(1)}, /*index=5*/bf16[...) while((s32[]{:T(128)}, f32[2048]{0:T(1024)S(1)}, ...), condition=%wide.region_9.10_spmd, body=%wide.region_7.9_spmd.sunk | while | flops 272104960 | bytes 1332415 | solution.py:43
  146.1 0.6 dynamic_slice.109
  147.5 2.1 fusion.44
  149.5 0.3 dynamic_update_slice.8
  149.8 0.6 dynamic_slice.109
  151.1 2.1 fusion.44
  153.2 0.3 dynamic_update_slice.8
  153.5 0.6 dynamic_slice.109
  154.8 2.1 fusion.44
  157.1 0.6 dynamic_slice.109
  158.4 2.1 fusion.44
  160.8 75.7 %psum.14 = f32[2048]{0:T(1024)S(1)} all-reduce(f32[2048]{0:T(1024)S(1)} %get-tuple-element.185), channel_id=1, replica_groups=mesh['imp'=32,'cre'=8] {'imp'}, use_global_device_ids=true, to_apply=%region_10.11 | all-reduce | flops 2048 | bytes 16384 | tf_op jit(solution)/shard_map/psum | solution.py:101
  236.7 66.0 %all-reduce.1 = f32[2048]{0:T(1024)S(1)} all-reduce(f32[2048]{0:T(1024)S(1)} %get-tuple-element.317), channel_id=1, replica_groups=mesh['imp'=32,'cre'=8] {'imp'}, use_global_device_ids=true, to_apply=%add.1 | all-reduce | flops 2048 | bytes 16384 | tf_op jit(solution)/shard_map/squeeze | solution.py:73
  302.8 15.2 %while.49 = (s32[]{:T(128)}, f32[1024]{0:T(1024)S(1)}, f32[1024]{0:T(1024)S(1)}, s32[4]{0:T(128)S(1)}, pred[1024,2048]{0,1:T(32,128)(4,1)S(1)}, /*index=5*/bf16[...) while((s32[]{:T(128)}, f32[1024]{0:T(1024)S(1)}, ...), condition=%wide.region_14.15_spmd.clone, body=%wide.region_11.14_spmd.clone.sunk | while | flops 273684480 | bytes 6075585 | solution.py:43
  302.8 0.6 dynamic_slice.123
  304.1 1.7 fusion.52
  305.8 0.8 select_reduce_fusion.5
  306.6 0.6 dynamic_slice.123
  307.9 1.7 fusion.52
  309.6 0.8 select_reduce_fusion.5
  310.4 0.6 dynamic_slice.123
  311.7 1.7 fusion.52
  313.4 0.8 select_reduce_fusion.5
  314.2 0.6 dynamic_slice.123
  315.5 1.7 fusion.52
  317.2 0.8 select_reduce_fusion.5
  318.0 12.5 %pmax.15 = f32[1024]{0:T(1024)S(1)} all-reduce(f32[1024]{0:T(1024)S(1)} %get-tuple-element.186), channel_id=1, replica_groups=mesh['imp'=32,'cre'=8] {'cre'}, use_global_device_ids=true, to_apply=%region_15.16 | all-reduce | flops 1024 | bytes 8192 | tf_op jit(solution)/shard_map/pmax | solution.py:81
  330.5 21.7 %all-gather.1 = f32[8192]{0:T(1024)S(1)} all-gather(f32[1024]{0:T(1024)S(1)} %exponential_multiply_fusion), channel_id=3, replica_groups=mesh['imp'=32,'cre'=8] {'cre'}, dimensions={0}, use_global_device_ids=true | all-gather | bytes 36864 | tf_op jit(solution)/shard_map/all_gather | solution.py:83
  352.2 14.6 %while.47 = (s32[]{:T(128)}, f32[2048]{0:T(1024)S(1)}, f32[1024]{0:T(1024)S(1)}, s32[4]{0:T(128)S(1)}, pred[1024,2048]{0,1:T(32,128)(4,1)S(1)}, /*index=5*/bf16[...) while((s32[]{:T(128)}, f32[2048]{0:T(1024)S(1)}, ...), condition=%wide.region_19.20_spmd, body=%wide.region_17.19_spmd.sunk | while | flops 272104960 | bytes 1332415 | solution.py:43
  352.2 0.6 dynamic_slice.113
  353.6 2.1 fusion.47
  355.9 0.6 dynamic_slice.113
  357.2 2.1 fusion.47
  359.3 0.3 dynamic_update_slice.9
  359.6 0.6 dynamic_slice.113
  360.9 2.1 fusion.47
  363.2 0.6 dynamic_slice.113
  364.5 2.1 fusion.47
  366.8 75.9 %psum.15 = f32[2048]{0:T(1024)S(1)} all-reduce(f32[2048]{0:T(1024)S(1)} %get-tuple-element.188), channel_id=1, replica_groups=mesh['imp'=32,'cre'=8] {'imp'}, use_global_device_ids=true, to_apply=%region_20.21 | all-reduce | flops 2048 | bytes 16384 | tf_op jit(solution)/shard_map/psum | solution.py:101
  442.7 0.6 multiply_add_fusion
  (64 shorter events, 3.2 us)
Async XLA Ops:
  7.2 85.4 %all-gather.4.cloned.1.call-start = ((), (), s32[]{:S(2)}) async-start(), calls=%async_computation | async-start | bytes 1081344 | tf_op jit(solution)/shard_map/all_gather | solution.py:95
  92.5 1.2 copy-start.3
  93.7 52.4 %copy-start.4 = (f32[1024]{0:T(1024)S(1)}, f32[1024]{0:T(1024)}, u32[]{:S(2)}) copy-start(f32[1024]{0:T(1024)} %param.19) | copy-start | bytes 12292
  146.1 90.4 %copy-start.1 = (f32[1,64]{1,0:T(1,128)S(1)}, f32[1,64]{1,0:T(1,128)}, u32[]{:S(2)}) copy-start(f32[1,64]{1,0:T(1,128)} %param.20) | copy-start | bytes 772
  146.1 90.4 %copy-start.2 = (f32[1,64]{1,0:T(1,128)S(1)}, f32[1,64]{1,0:T(1,128)}, u32[]{:S(2)}) copy-start(f32[1,64]{1,0:T(1,128)} %param.21) | copy-start | bytes 772
  366.8 76.5 %copy-start = (f32[1024]{0:T(1024)}, f32[1024]{0:T(1024)S(1)}, u32[]{:S(2)}) copy-start(f32[1024]{0:T(1024)S(1)} %get-tuple-element.705) | copy-start | bytes 12292
Sparse Core Ops, SparseCore 0:
  10.8 81.6 all-gather.3
